TPU v7x, 32 devices: a whole 2x2x4 slice. The times are simulated.
32 devices in a mesh: row: 4 (over z), col: 8 (over y, x, core).
Axes of the slice: x: 2, y: 2, z: 4, core: 2. Of those that a mesh axis runs over, the one named last changes fastest.
Arguments:
- spectra: bfloat16 [1024, 32, 128], P(('row', 'col')), may hold values from -6 to 6
- pair_bins: int32 [1024, 1024], P('row', 'col'), may hold values from 0 to 255
- row_subs: int32 [4, 16], P('row'), may hold values from 0 to 31, as said below
- station_subs: int32 [1024, 8], replicated, may hold values from 0 to 31, as said below
- kernel: bfloat16 [32, 256, 256], replicated, may hold values from -0.375 to 0.375
Outputs:
- spectrum: float32 [32, 32, 256], P(('row', 'col'))
Inputs may be any that keep to these rules, and one draw needn't show every extreme that they name: `row_subs`: each row lists 16 distinct subarrays; each subarray is listed for exactly two row blocks. `station_subs`: each station names 8 distinct subarrays, all listed in row_subs for the station's row block.
All inputs are finite; a program needn't handle non-finite values.
Results may differ from a plain program's by a relative error of at most 0.0039.
Values may be sent and summed in bfloat16 or wider, within the bound.
A program may use at most 64 MiB of HBM per device.

v0:
```python
import math
import jax
import jax.numpy as jnp
from jax import lax
from jax.sharding import PartitionSpec as P

F = 32
NBIN = 256
SUB_DEV = 1


def spread_rows(slot_terms, slot_subs, row_count):
    targets = jnp.arange(row_count, dtype=jnp.int32)
    selector = (targets[:, None] == slot_subs[None, :]).astype(jnp.float32)
    return jnp.dot(selector, slot_terms, precision=lax.Precision.HIGHEST)


def project(owned_bins, kernel):
    velocity_power = jnp.einsum(
        "sfb,fbv->sfv", owned_bins, kernel, preferred_element_type=jnp.float32
    )
    scale = lax.rsqrt(jnp.mean(velocity_power * velocity_power, axis=2, keepdims=True) + 1e-06)
    return velocity_power * scale


def on_device(spectra, pair_bins, row_subs, station_subs, kernel):
    shard_rows = spectra.shape[0]
    col_total = lax.axis_size("col")
    row_index = lax.axis_index("row")
    col_index = lax.axis_index("col")
    row_spectra = lax.all_gather(spectra, "col", axis=0, tiled=True)
    col_spectra = lax.all_gather(spectra, "row", axis=0, tiled=True)
    row_span = row_spectra.shape[0]
    col_span = col_spectra.shape[0]
    slot_subs = row_subs[0]
    slot_count = slot_subs.shape[0]
    row_members = lax.dynamic_slice_in_dim(station_subs, row_index * row_span, row_span, 0)
    positions = jnp.arange(col_span, dtype=jnp.int32)
    col_ids = (
        positions // shard_rows * col_total + col_index
    ) * shard_rows + positions % shard_rows
    col_members = jnp.take(station_subs, col_ids, axis=0)
    row_mask = jnp.any(row_members[None, :, :] == slot_subs[:, None, None], axis=2).astype(
        jnp.bfloat16
    )
    col_mask = jnp.any(col_members[None, :, :] == slot_subs[:, None, None], axis=2).astype(
        jnp.bfloat16
    )
    cross_spec = jnp.einsum(
        "aft,jft->faj", row_spectra, col_spectra, preferred_element_type=jnp.float32
    ).astype(jnp.bfloat16)
    step_rows = math.gcd(row_span, max(1, 2048 // col_span))
    step_count = row_span // step_rows
    bin_ids = jnp.arange(NBIN, dtype=jnp.int32)

    def accumulate(step_index, running):
        first_row = step_index * step_rows
        cross_part = lax.dynamic_slice_in_dim(cross_spec, first_row, step_rows, 1)
        mask_part = lax.dynamic_slice_in_dim(row_mask, first_row, step_rows, 1)
        bins_part = lax.dynamic_slice_in_dim(pair_bins, first_row, step_rows, 0)
        weighted = mask_part[:, None, :, None] * col_mask[:, None, None, :] * cross_part[None]
        onehot = (bins_part.reshape(-1, 1) == bin_ids[None, :]).astype(jnp.bfloat16)
        return running + jnp.dot(
            weighted.reshape(slot_count * F, step_rows * col_span),
            onehot,
            preferred_element_type=jnp.float32,
        )

    partial_value = lax.fori_loop(
        0, step_count, accumulate, jnp.zeros((slot_count * F, NBIN), jnp.float32)
    )
    partial_value = partial_value.reshape(slot_count, F, NBIN)
    freq_part = lax.psum_scatter(partial_value, "col", scatter_dimension=1, tiled=True)
    freq_share = freq_part.shape[1]
    group_rows = SUB_DEV * col_total
    summed = lax.psum_scatter(
        spread_rows(
            freq_part.reshape(slot_count, freq_share * NBIN),
            slot_subs,
            lax.axis_size("row") * group_rows,
        ),
        "row",
        scatter_dimension=0,
        tiled=True,
    )
    binned = summed.reshape(group_rows, freq_share, NBIN).astype(jnp.bfloat16)
    return project(lax.all_to_all(binned, "col", split_axis=0, concat_axis=1, tiled=True), kernel)


def solution(mesh):
    in_specs = (P(("row", "col"), None, None), P("row", "col"), P("row", None), P(), P())
    out_specs = P(("row", "col"), None, None)
    return jax.shard_map(
        on_device, mesh=mesh, in_specs=in_specs, out_specs=out_specs, check_vma=False
    )
```

profile of v0, /device:TPU:0, one launch (start us, length us, event | category | flops | bytes accessed | tf_op | source)
XLA Modules:
  0.0 180.9 jit_solution(14719300169441912463)
XLA Ops:
  6.5 1.8 copy.29
  12.6 27.1 %all-gather.5.cloned.1.call-done = bf16[128,32,128]{2,0,1:T(8,128)(2,1)} async-done(((bf16[32,32,128]{2,0,1:T(8,128)(2,1)}), bf16[128,32,128]{2,0,1:T(8,128)(2,1)}) %all-gather.5.cloned.1.call-update) | async-done | bytes 1048592 | tf_op jit(solution)/shard_map/all_gather | solution.py:32
  39.6 29.4 %all-gather.3.cloned.1.call-done = bf16[256,32,128]{2,0,1:T(8,128)(2,1)} async-done(((bf16[32,32,128]{2,0,1:T(8,128)(2,1)}), bf16[256,32,128]{2,0,1:T(8,128)(2,1)}) %all-gather.3.cloned.1.call-update) | async-done | bytes 2097168 | tf_op jit(solution)/shard_map/all_gather | solution.py:31
  69.0 2.6 %convolution_convert_fusion = bf16[32,256,128]{2,1,0:T(8,128)(2,1)S(1)} fusion(bf16[256,32,128]{2,0,1:T(8,128)(2,1)} %all-gather.3.cloned.1.call-done, bf16[128,32,128]{2,0,1:T(8,128)(2,1)} %all-gather.5.cloned.1.call-done), kind=kOutput, calls=%fused_computation.13 | convolution fusion | flops 269484032 | bytes 5242880 | tf_op jit(solution)/shard_map/aft,jft->faj/dot_general | solution.py:49
  71.6 33.1 %while.14 = (s32[]{:T(128)}, f32[512,256]{1,0:T(8,128)S(1)}, bf16[16,256]{1,0:T(8,128)(2,1)S(1)}, bf16[16,128]{1,0:T(8,128)(2,1)S(1)}, bf16[32,256,128]{2,1,0:T(...) while((s32[]{:T(128)}, f32[512,256]{1,0:T(8,128)S(1)}, ...), condition=%wide.region_3.4_spmd.clone, body=%wide.region_2.3_spmd.clone.sunk | while | flops 538738688 | bytes 5797553 | solution.py:69
  72.7 1.0 fusion.31
  74.8 1.0 fusion.31
  76.8 1.0 fusion.31
  78.9 1.0 fusion.31
  81.0 1.0 fusion.31
  83.0 1.0 fusion.31
  85.1 1.0 fusion.31
  87.2 1.0 fusion.31
  89.3 1.0 fusion.31
  93.4 1.0 fusion.31
  95.5 1.0 fusion.31
  99.6 1.0 fusion.31
  101.7 1.0 fusion.31
  103.8 1.0 fusion.31
  104.8 1.1 copy.31
  105.9 34.2 %reduce-scatter.3.cloned.1.call-done = f32[16,4,256]{2,0,1:T(8,128)} async-done(((f32[16,32,256]{2,0,1:T(8,128)}), f32[16,4,256]{2,0,1:T(8,128)}) %reduce-scatter.3.cloned.1.call-update) | async-done | bytes 65552 | tf_op jit(solution)/shard_map/reduce_scatter | solution.py:73
  141.9 19.9 %reduce-scatter.5.cloned.1.call-done = f32[8,1024]{1,0:T(8,128)} async-done(((f32[32,1024]{1,0:T(8,128)}), f32[8,1024]{1,0:T(8,128)}) %reduce-scatter.5.cloned.1.call-update) | async-done | bytes 32784 | tf_op jit(solution)/shard_map/reduce_scatter | solution.py:76
  162.5 8.2 %all_to_all.4 = bf16[8,4,256]{2,1,0:T(4,128)(2,1)S(1)} all-to-all(bf16[8,4,256]{2,1,0:T(4,128)(2,1)S(1)} %copy.33), channel_id=1, replica_groups=mesh['row'=4,'col'=8] {'col'}, dimensions={0} | all-to-all | bytes 32768 | tf_op jit(solution)/shard_map/all_to_all | solution.py:87
  170.7 2.8 %fusion.22 = f32[32,1,256]{2,1,0:T(1,128)S(1)} fusion(bf16[32,256,1]{1,2,0:T(2,128)(2,1)S(1)} %reshape.159, bf16[32,256,256]{2,1,0:T(8,128)(2,1)} %param.11), kind=kOutput, calls=%fused_computation.49 | convolution fusion | flops 4194304 | bytes 4243456 | tf_op jit(solution)/shard_map/sfb,fbv->sfv/dot_general | solution.py:19
  (113 shorter events, 26.2 us)
Async XLA Ops:
  6.5 5.9 %copy-start = (s32[1,16]{1,0:T(1,128)S(1)}, s32[1,16]{1,0:T(1,128)}, u32[]{:S(2)}) copy-start(s32[1,16]{1,0:T(1,128)} %param.9) | copy-start | bytes 196
  6.5 33.1 %all-gather.5.cloned.1.call-start = ((), (), s32[]{:S(2)}) async-start(), calls=%async_computation.4 | async-start | bytes 1310720 | tf_op jit(solution)/shard_map/all_gather | solution.py:32
  8.3 60.7 %all-gather.3.cloned.1.call-start = ((), (), s32[]{:S(2)}) async-start(), calls=%async_computation.3 | async-start | bytes 2359296 | tf_op jit(solution)/shard_map/all_gather | solution.py:31
  9.1 131.1 %reduce-scatter.3.cloned.1.call-start = ((), (), s32[]{:S(2)}) async-start(), calls=%async_computation.5 | async-start | bytes 589824 | tf_op jit(solution)/shard_map/reduce_scatter | solution.py:73
  105.9 55.8 %reduce-scatter.5.cloned.1.call-start = ((), (), s32[]{:S(2)}) async-start(), calls=%async_computation.6 | async-start | bytes 163840 | tf_op jit(solution)/shard_map/reduce_scatter | solution.py:76
Sparse Core Ops, SparseCore 0:
  8.9 30.6 all-gather.4
  41.5 27.4 all-gather.2
  106.0 34.1 reduce-scatter.2
  142.3 19.4 reduce-scatter.4
where the time goes:
time: 182 us; the launch traced here: 181 us
  waiting for transfers between devices  111 us (61%)
  matrix products  21.9 us (12%)
  local copies, waits for them, and re-layouts  19 us (10%)
  between operations  13.2 us (7%)
  blocking collectives  8.21 us (5%)
  other arithmetic  6.36 us (3%)
    reduce_scatter x1, waiting for transfers between devices, on_device(): lax.psum_scatter(partial_value, 'col', scatter_dimension=1, tiled=True)  34.2 us
    all_gather x1, waiting for transfers between devices, on_device(): row_spectra = lax.all_gather(spectra, 'col', axis=0, tiled=True)  29.4 us
    all_gather x1, waiting for transfers between devices, on_device(): col_spectra = lax.all_gather(spectra, 'row', axis=0, tiled=True)  27.1 us
    reduce_scatter x1, waiting for transfers between devices, on_device(): lax.psum_scatter(spread_rows(freq_part.reshape(slot_count, freq_share * N...  19.9 us
    dot_general x16, matrix products, accumulate(): jnp.dot(weighted.reshape(slot_count * F, step_rows * col_span), onehot, p...  15.6 us
    eq x16, local copies, waits for them, and re-layouts, accumulate(): onehot = (bins_part.reshape(-1, 1) == bin_ids[None, :]).astype(jnp.bfloat16)  11.2 us
    all_to_all x1, blocking collectives, on_device(): lax.all_to_all(binned, 'col', split_axis=0, concat_axis=1, tiled=True)  8.21 us
    mul x32, other arithmetic, accumulate(): mask_part[:, None, :, None] * col_mask[:, None, None, :] * cross_part[None]  3.76 us
  transfers between devices with their start and end apart: 4, of which 4 were waited for; matrix products, arithmetic and copies ran while one was open for 2% of the time, Pallas kernels for 0%

commit v1 on v0

--- a/solution.py
+++ b/solution.py
@@ -28,7 +28,12 @@
     col_total = lax.axis_size("col")
     row_index = lax.axis_index("row")
     col_index = lax.axis_index("col")
-    row_spectra = lax.all_gather(spectra, "col", axis=0, tiled=True)
+    ring = [spectra]
+    for hop in range(7):
+        ring.append(lax.ppermute(ring[-1], "col", [(dev, (dev + 1) % 8) for dev in range(8)]))
+    row_spectra = jnp.roll(
+        jnp.concatenate(ring[::-1], axis=0), (lax.axis_index("col") + 1) * ring[0].shape[0], axis=0
+    )
     col_spectra = lax.all_gather(spectra, "row", axis=0, tiled=True)
     row_span = row_spectra.shape[0]
     col_span = col_spectra.shape[0]

time: 182 us -> 198 us (1.088)
  local copies, waits for them, and re-layouts: 19 us -> 45.6 us
  waiting for transfers between devices: 111 us -> 98.4 us
    ppermute x0 -> x7, waiting for transfers between devices: none -> 42.9 us  [on_device(): lax.ppermute(ring[-1], 'col', [(dev, (dev + 1) % 8) for dev in range(8)])]
    all_gather x1 -> x0, waiting for transfers between devices: 29.4 us -> none  [on_device(): row_spectra = lax.all_gather(spectra, 'col', axis=0, tiled=True)]
    all_gather x1, waiting for transfers between devices: 27.1 us -> 0.01 us  [on_device(): col_spectra = lax.all_gather(spectra, 'row', axis=0, tiled=True)]
    dynamic_slice x16, local copies, waits for them, and re-layouts: 0.43 us -> 14.9 us  [accumulate(): cross_part = lax.dynamic_slice_in_dim(cross_spec, first_row, step_rows, 1)]
    unnamed x4 -> x23, local copies, waits for them, and re-layouts: 2.74 us -> 14 us
  transfers between devices with their start and end apart: 4 -> 10, of which waited for: 4 -> 9; matrix products, arithmetic and copies ran while one was open for 2% -> 9% of each run, Pallas kernels for 0% -> 0%
where the time goes in v1:
time: 198 us; the launch traced here: 197 us
  waiting for transfers between devices  98.4 us (50%)
  local copies, waits for them, and re-layouts  45.6 us (23%)
  matrix products  23.1 us (12%)
  between operations  13.2 us (7%)
  blocking collectives  8.15 us (4%)
  other arithmetic  7.06 us (4%)
    ppermute x7, waiting for transfers between devices, on_device(): lax.ppermute(ring[-1], 'col', [(dev, (dev + 1) % 8) for dev in range(8)])  42.9 us
    reduce_scatter x1, waiting for transfers between devices, on_device(): lax.psum_scatter(partial_value, 'col', scatter_dimension=1, tiled=True)  35.3 us
    reduce_scatter x1, waiting for transfers between devices, on_device(): lax.psum_scatter(spread_rows(freq_part.reshape(slot_count, freq_share * N...  20.1 us
    dot_general x16, matrix products, accumulate(): jnp.dot(weighted.reshape(slot_count * F, step_rows * col_span), onehot, p...  15.6 us
    dynamic_slice x16, local copies, waits for them, and re-layouts, accumulate(): cross_part = lax.dynamic_slice_in_dim(cross_spec, first_row, step_rows, 1)  14.9 us
    unnamed x23, local copies, waits for them, and re-layouts  14 us
    eq x16, local copies, waits for them, and re-layouts, accumulate(): onehot = (bins_part.reshape(-1, 1) == bin_ids[None, :]).astype(jnp.bfloat16)  11.3 us
    all_to_all x1, blocking collectives, on_device(): lax.all_to_all(binned, 'col', split_axis=0, concat_axis=1, tiled=True)  8.15 us
  transfers between devices with their start and end apart: 10, of which 9 were waited for; matrix products, arithmetic and copies ran while one was open for 9% of the time, Pallas kernels for 0%

profile of v1, /device:TPU:0, one launch (start us, length us, event | category | flops | bytes accessed | tf_op | source)
XLA Modules:
  0.0 196.9 jit_solution(11725139641559954471)
XLA Ops:
  6.5 1.1 copy.37
  8.2 6.9 %collective-permute-done = bf16[32,32,128]{2,0,1:T(8,128)(2,1)S(1)} collective-permute-done((bf16[32,32,128]{2,0,1:T(8,128)(2,1)S(1)}, bf16[32,32,128]{2,0,1:T(8,128)(2,1)S(1)}, u32[]{:S(2)}, u32[]{:S(2)}) %collective-permute-start) | collective-permute-done | bytes 262176 | tf_op jit(solution)/shard_map/ppermute | solution.py:33
  15.1 6.7 %collective-permute-done.1 = bf16[32,32,128]{2,0,1:T(8,128)(2,1)S(1)} collective-permute-done((bf16[32,32,128]{2,0,1:T(8,128)(2,1)S(1)}, bf16[32,32,128]{2,0,1:T(8,128)(2,1)S(1)}, u32[]{:S(2)}, u32[]{:S(2)}) %collective-permute-start.1) | collective-permute-done | bytes 262176 | tf_op jit(solution)/shard_map/ppermute | solution.py:33
  21.8 6.7 %collective-permute-done.2 = bf16[32,32,128]{2,0,1:T(8,128)(2,1)S(1)} collective-permute-done((bf16[32,32,128]{2,0,1:T(8,128)(2,1)S(1)}, bf16[32,32,128]{2,0,1:T(8,128)(2,1)S(1)}, u32[]{:S(2)}, u32[]{:S(2)}) %collective-permute-start.2) | collective-permute-done | bytes 262176 | tf_op jit(solution)/shard_map/ppermute | solution.py:33
  28.5 6.7 %collective-permute-done.3 = bf16[32,32,128]{2,0,1:T(8,128)(2,1)S(1)} collective-permute-done((bf16[32,32,128]{2,0,1:T(8,128)(2,1)S(1)}, bf16[32,32,128]{2,0,1:T(8,128)(2,1)S(1)}, u32[]{:S(2)}, u32[]{:S(2)}) %collective-permute-start.3) | collective-permute-done | bytes 262176 | tf_op jit(solution)/shard_map/ppermute | solution.py:33
  36.8 5.1 %collective-permute-done.4 = bf16[32,32,128]{2,0,1:T(8,128)(2,1)S(1)} collective-permute-done((bf16[32,32,128]{2,0,1:T(8,128)(2,1)S(1)}, bf16[32,32,128]{2,0,1:T(8,128)(2,1)S(1)}, u32[]{:S(2)}, u32[]{:S(2)}) %collective-permute-start.4) | collective-permute-done | bytes 262176 | tf_op jit(solution)/shard_map/ppermute | solution.py:33
  43.6 5.0 %collective-permute-done.5 = bf16[32,32,128]{2,0,1:T(8,128)(2,1)S(1)} collective-permute-done((bf16[32,32,128]{2,0,1:T(8,128)(2,1)S(1)}, bf16[32,32,128]{2,0,1:T(8,128)(2,1)S(1)}, u32[]{:S(2)}, u32[]{:S(2)}) %collective-permute-start.5) | collective-permute-done | bytes 262176 | tf_op jit(solution)/shard_map/ppermute | solution.py:33
  49.6 5.8 %collective-permute-done.6 = bf16[32,32,128]{2,0,1:T(8,128)(2,1)S(1)} collective-permute-done((bf16[32,32,128]{2,0,1:T(8,128)(2,1)S(1)}, bf16[32,32,128]{2,0,1:T(8,128)(2,1)S(1)}, u32[]{:S(2)}, u32[]{:S(2)}) %collective-permute-start.6) | collective-permute-done | bytes 262176 | tf_op jit(solution)/shard_map/ppermute | solution.py:33
  68.1 3.9 %fusion.11 = bf16[32,256,128]{2,1,0:T(8,128)(2,1)} fusion(bf16[128,32,128]{2,0,1:T(8,128)(2,1)} %all-gather.2.cloned.1.call-done, bf16[512,32,128]{2,0,1:T(8,128)(2,1)} %constant_dynamic-update-slice_fusion, s32[]{:T(128)S(6)} %select_n.90), kind=kOutput, calls=%fused_computation.15 | convolution fusion | flops 269484032 | bytes 5242884 | tf_op jit(solution)/shard_map/aft,jft->faj/dot_general | solution.py:54
  72.0 47.5 %while.14 = (s32[]{:T(128)}, f32[512,256]{1,0:T(8,128)S(1)}, bf16[16,256]{1,0:T(8,128)(2,1)S(1)}, bf16[16,128]{1,0:T(8,128)(2,1)S(1)}, bf16[32,256,128]{2,1,0:T(...) while((s32[]{:T(128)}, f32[512,256]{1,0:T(8,128)S(1)}, ...), condition=%wide.region_3.4_spmd.clone, body=%wide.region_2.3_spmd.clone.sunk | while | flops 538738688 | bytes 5797545 | solution.py:74
  73.9 1.0 fusion.36
  76.9 1.0 fusion.36
  79.9 1.0 fusion.36
  82.8 1.0 fusion.36
  85.8 1.0 fusion.36
  91.8 1.0 fusion.36
  97.7 1.0 fusion.36
  112.6 1.0 fusion.36
  118.5 1.0 fusion.36
  119.5 1.1 copy.41
  120.7 35.3 %reduce-scatter.3.cloned.1.call-done = f32[16,4,256]{2,0,1:T(8,128)} async-done(((f32[16,32,256]{2,0,1:T(8,128)}), f32[16,4,256]{2,0,1:T(8,128)}) %reduce-scatter.3.cloned.1.call-update) | async-done | bytes 65552 | tf_op jit(solution)/shard_map/reduce_scatter | solution.py:78
  157.7 20.1 %reduce-scatter.5.cloned.1.call-done = f32[8,1024]{1,0:T(8,128)} async-done(((f32[32,1024]{1,0:T(8,128)}), f32[8,1024]{1,0:T(8,128)}) %reduce-scatter.5.cloned.1.call-update) | async-done | bytes 32784 | tf_op jit(solution)/shard_map/reduce_scatter | solution.py:81
  178.6 8.2 %all_to_all.4 = bf16[8,4,256]{2,1,0:T(4,128)(2,1)S(1)} all-to-all(bf16[8,4,256]{2,1,0:T(4,128)(2,1)S(1)} %copy.43), channel_id=1, replica_groups=mesh['row'=4,'col'=8] {'col'}, dimensions={0} | all-to-all | bytes 32768 | tf_op jit(solution)/shard_map/all_to_all | solution.py:92
  186.7 2.8 %fusion.28 = f32[32,1,256]{2,1,0:T(1,128)S(1)} fusion(bf16[32,256,1]{1,2,0:T(2,128)(2,1)S(1)} %reshape.159, bf16[32,256,256]{2,1,0:T(8,128)(2,1)} %param.11), kind=kOutput, calls=%fused_computation.68 | convolution fusion | flops 4194304 | bytes 4243456 | tf_op jit(solution)/shard_map/sfb,fbv->sfv/dot_general | solution.py:19
  (144 shorter events, 58.8 us)
Async XLA Ops:
  6.5 54.3 %copy-start = (bf16[32,32,128]{2,1,0:T(8,128)(2,1)S(1)}, bf16[32,32,128]{2,1,0:T(8,128)(2,1)}, u32[]{:S(2)}) copy-start(bf16[32,32,128]{2,1,0:T(8,128)(2,1)} %param.7) | copy-start | bytes 786436
  6.5 61.5 %all-gather.2.cloned.1.call-start = ((), (), s32[]{:S(2)}) async-start(), calls=%async_computation.3 | async-start | bytes 1310720 | tf_op jit(solution)/shard_map/all_gather | solution.py:37
  7.7 27.6 %copy-start.1 = (bf16[32,32,128]{2,0,1:T(8,128)(2,1)}, bf16[32,32,128]{2,0,1:T(8,128)(2,1)S(1)}, u32[]{:S(2)}) copy-start(bf16[32,32,128]{2,0,1:T(8,128)(2,1)S(1)} %copy.37) | copy-start | bytes 786436
  7.7 7.5 %collective-permute-start = (bf16[32,32,128]{2,0,1:T(8,128)(2,1)S(1)}, bf16[32,32,128]{2,0,1:T(8,128)(2,1)S(1)}, u32[]{:S(2)}, u32[]{:S(2)}) collective-permute-start(bf16[32,32,128]{2,0,1:T(8,128)(2,1)S(1)} %copy.37), channel_id=1, source_target_pairs={{0,1},{1,2},{2,3},{3,4},{4,5},{5,6},{6,7},{7,0},{8,9},{9,10},{10,1... | collective-permute-start | bytes 786440 | tf_op jit(solution)/shard_map/ppermute | solution.py:33
  15.1 6.7 %collective-permute-start.1 = (bf16[32,32,128]{2,0,1:T(8,128)(2,1)S(1)}, bf16[32,32,128]{2,0,1:T(8,128)(2,1)S(1)}, u32[]{:S(2)}, u32[]{:S(2)}) collective-permute-start(bf16[32,32,128]{2,0,1:T(8,128)(2,1)S(1)} %collective-permute-done), channel_id=1, source_target_pairs={{0,1},{1,2},{2,3},{3,4},{4,5},{5,6},{6,7},{7,0},{8,9},{9,10},{10,1... | collective-permute-start | bytes 786440 | tf_op jit(solution)/shard_map/ppermute | solution.py:33
  21.8 6.7 %collective-permute-start.2 = (bf16[32,32,128]{2,0,1:T(8,128)(2,1)S(1)}, bf16[32,32,128]{2,0,1:T(8,128)(2,1)S(1)}, u32[]{:S(2)}, u32[]{:S(2)}) collective-permute-start(bf16[32,32,128]{2,0,1:T(8,128)(2,1)S(1)} %collective-permute-done.1), channel_id=1, source_target_pairs={{0,1},{1,2},{2,3},{3,4},{4,5},{5,6},{6,7},{7,0},{8,9},{9,10},{10,1... | collective-permute-start | bytes 786440 | tf_op jit(solution)/shard_map/ppermute | solution.py:33
  28.5 6.7 %collective-permute-start.3 = (bf16[32,32,128]{2,0,1:T(8,128)(2,1)S(1)}, bf16[32,32,128]{2,0,1:T(8,128)(2,1)S(1)}, u32[]{:S(2)}, u32[]{:S(2)}) collective-permute-start(bf16[32,32,128]{2,0,1:T(8,128)(2,1)S(1)} %collective-permute-done.2), channel_id=1, source_target_pairs={{0,1},{1,2},{2,3},{3,4},{4,5},{5,6},{6,7},{7,0},{8,9},{9,10},{10,1... | collective-permute-start | bytes 786440 | tf_op jit(solution)/shard_map/ppermute | solution.py:33
  35.2 6.7 %collective-permute-start.4 = (bf16[32,32,128]{2,0,1:T(8,128)(2,1)S(1)}, bf16[32,32,128]{2,0,1:T(8,128)(2,1)S(1)}, u32[]{:S(2)}, u32[]{:S(2)}) collective-permute-start(bf16[32,32,128]{2,0,1:T(8,128)(2,1)S(1)} %collective-permute-done.3), channel_id=1, source_target_pairs={{0,1},{1,2},{2,3},{3,4},{4,5},{5,6},{6,7},{7,0},{8,9},{9,10},{10,1... | collective-permute-start | bytes 786440 | tf_op jit(solution)/shard_map/ppermute | solution.py:33
  35.3 120.7 %reduce-scatter.3.cloned.1.call-start = ((), (), s32[]{:S(2)}) async-start(), calls=%async_computation.4 | async-start | bytes 589824 | tf_op jit(solution)/shard_map/reduce_scatter | solution.py:78
  41.9 6.7 %collective-permute-start.5 = (bf16[32,32,128]{2,0,1:T(8,128)(2,1)S(1)}, bf16[32,32,128]{2,0,1:T(8,128)(2,1)S(1)}, u32[]{:S(2)}, u32[]{:S(2)}) collective-permute-start(bf16[32,32,128]{2,0,1:T(8,128)(2,1)S(1)} %collective-permute-done.4), channel_id=1, source_target_pairs={{0,1},{1,2},{2,3},{3,4},{4,5},{5,6},{6,7},{7,0},{8,9},{9,10},{10,1... | collective-permute-start | bytes 786440 | tf_op jit(solution)/shard_map/ppermute | solution.py:33
  48.6 6.7 %collective-permute-start.6 = (bf16[32,32,128]{2,0,1:T(8,128)(2,1)S(1)}, bf16[32,32,128]{2,0,1:T(8,128)(2,1)S(1)}, u32[]{:S(2)}, u32[]{:S(2)}) collective-permute-start(bf16[32,32,128]{2,0,1:T(8,128)(2,1)S(1)} %collective-permute-done.5), channel_id=1, source_target_pairs={{0,1},{1,2},{2,3},{3,4},{4,5},{5,6},{6,7},{7,0},{8,9},{9,10},{10,1... | collective-permute-start | bytes 786440 | tf_op jit(solution)/shard_map/ppermute | solution.py:33
  72.0 84.9 %copy-start.2 = (s32[1,16]{1,0:T(1,128)S(1)}, s32[1,16]{1,0:T(1,128)}, u32[]{:S(2)}) copy-start(s32[1,16]{1,0:T(1,128)} %param.9) | copy-start | bytes 196
  120.6 57.2 %reduce-scatter.5.cloned.1.call-start = ((), (), s32[]{:S(2)}) async-start(), calls=%async_computation.5 | async-start | bytes 163840 | tf_op jit(solution)/shard_map/reduce_scatter | solution.py:81
Sparse Core Ops, SparseCore 0:
  35.4 30.2 all-gather.1
  120.7 35.2 reduce-scatter.2
  158.2 19.4 reduce-scatter.4
